TPU v7x, 256 devices: a whole 4x4x8 slice. The times are simulated.
256 devices in a mesh: sub: 8 (over z), row: 2 (over core), col: 16 (over y, x).
Axes of the slice: x: 4, y: 4, z: 8, core: 2. Of those that a mesh axis runs over, the one named last changes fastest.
Arguments:
- factor_cols: bfloat16 [8, 2, 2048, 4096], P('sub', None, 'col', 'row'), may hold values from -0.09375 to 0.09375
- block_pattern: int32 [8, 16, 16], P('sub'), may hold values 0 or 1
- diag_inverse: float32 [8, 4096, 2048], P('sub', ('row', 'col')), may hold values from -1 to 2
- coupling_cols: bfloat16 [8, 2, 2048, 1024], P('sub', 'row', 'col'), may hold values from -0.09375 to 0.09375
- separator_rows: int32 [8, 1024], P('sub'), may hold values from 0 to 1535, as said below
- root_inverse: float32 [1536, 1536], P('col'), may hold values from -1 to 2
- right_side: float32 [8, 4096, 128], P('sub', 'row'), may hold values from -6 to 6
- root_right: float32 [1536, 128], P('col'), may hold values from -6 to 6
Outputs:
- solution: float32 [8, 4096, 128], P('sub', ('row', 'col'))
- root_solution: float32 [1536, 128], P('col')
Inputs may be any that keep to these rules, and one draw needn't show every extreme that they name: `separator_rows`: within one section the 1024 entries are distinct.
All inputs are finite; a program needn't handle non-finite values. No bound on the sum of `block_pattern` on one device may be relied on, other than what follows from the above.
Results may differ from a plain program's by a relative error of at most 0.003.
Values may be sent and summed in bfloat16 or wider, within the bound.
No kernel may reach another device: no remote copies, remote signals or barrier semaphores. Data moves between devices by JAX's collectives and lax.ppermute only.
A program may use at most 64 MiB of HBM per device.

v0:
```python
import jax
import jax.numpy as jnp
from jax import lax
from jax.sharding import PartitionSpec as P

BLOCK = 256
SEPARATOR = 1536
precise = lax.Precision.HIGHEST
first_axes = (((0,), (0,)), ((), ()))


def spread(block, axis, source):
    block = jnp.where(lax.axis_index(axis) == source, block, jnp.zeros_like(block))
    return lax.psum(block, axis)


def shards(
    factor_cols,
    block_pattern,
    diag_inverse,
    coupling_cols,
    separator_rows,
    root_inverse,
    right_side,
    root_right,
):
    factor = factor_cols[0]
    table = block_pattern[0]
    inverse = diag_inverse[0]
    couple_own = coupling_cols[0, 0]
    right_rows = right_side[0]
    rows_sep = separator_rows[0]
    panel_count, col_width, panel_rows = factor.shape
    sources = right_rows.shape[1]
    block_count = table.shape[1]
    row_id = lax.axis_index("row")
    col_id = lax.axis_index("col")
    sub_id = lax.axis_index("sub")
    own_blocks = lax.dynamic_slice_in_dim(
        table, row_id * (panel_rows // BLOCK), panel_rows // BLOCK, 0
    ).astype(jnp.float32)
    row_mask = jnp.repeat(own_blocks, BLOCK, axis=0)
    col_pos = (
        jnp.arange(panel_count)[:, None] * panel_rows
        + col_id * col_width
        + jnp.arange(col_width)[None, :]
    )
    selector = (jnp.arange(block_count)[:, None, None] == (col_pos // BLOCK)[None]).astype(
        jnp.float32
    )
    pattern_mask = jnp.einsum("in,nqj->qji", row_mask, selector)
    below_mask = (jnp.arange(panel_count) < row_id).astype(jnp.float32)[:, None, None]
    masked = factor * (pattern_mask * below_mask).astype(jnp.bfloat16)
    zero_panel = jnp.zeros((panel_rows, sources), jnp.float32)
    zero_share = jnp.zeros((col_width, sources), jnp.float32)

    def forward(current, carried):
        accumulated, solved = carried
        panel_total = lax.psum(accumulated, "col")
        solved = lax.cond(
            row_id == current,
            lambda values: jnp.dot(
                inverse, right_rows - values, precision=precise, preferred_element_type=jnp.float32
            ),
            lambda values: solved,
            panel_total,
        )
        received = spread(solved.astype(jnp.bfloat16), "row", current)
        factor_now = lax.dynamic_index_in_dim(masked, current, 0, keepdims=False)
        accumulated = accumulated + lax.dot_general(
            factor_now, received, first_axes, preferred_element_type=jnp.float32
        )
        return (accumulated, solved)

    accumulated, solved = lax.fori_loop(0, panel_count, forward, (zero_panel, zero_share))
    own_low = solved.astype(jnp.bfloat16)
    sep_partial = lax.dot_general(
        couple_own, own_low, first_axes, preferred_element_type=jnp.float32
    )
    onehot = (jnp.arange(SEPARATOR)[:, None] == rows_sep[None, :]).astype(jnp.float32)
    mapped = jnp.dot(onehot, sep_partial, precision=precise, preferred_element_type=jnp.float32)
    share_rows = root_inverse.shape[0]
    slice_start = col_id * share_rows
    first_device = ((sub_id == 0) & (row_id == 0)).astype(jnp.float32)
    own_rows = (
        lax.dynamic_slice_in_dim(-mapped, slice_start, share_rows, 0) + first_device * root_right
    )
    root_term = lax.dynamic_update_slice_in_dim(-mapped, own_rows, slice_start, 0)
    root_rhs = lax.psum(root_term, ("sub", "row", "col"))
    root_half = jnp.dot(
        root_inverse, root_rhs, precision=precise, preferred_element_type=jnp.float32
    )
    root_part = lax.psum_scatter(
        lax.dot_general(
            root_inverse,
            root_half,
            first_axes,
            precision=precise,
            preferred_element_type=jnp.float32,
        ),
        "col",
        scatter_dimension=0,
        tiled=True,
    )
    root_full = lax.all_gather(root_part.astype(jnp.bfloat16), "col", axis=0, tiled=True).astype(
        root_part.dtype
    )
    picked = lax.dot_general(
        onehot, root_full, first_axes, precision=precise, preferred_element_type=jnp.float32
    ).astype(jnp.bfloat16)
    couple_back = jnp.dot(couple_own, picked, preferred_element_type=jnp.float32)

    def backward(counter, carried):
        finished, panel_low = carried
        current = panel_count - 1 - counter
        factor_now = lax.dynamic_index_in_dim(masked, current, 0, keepdims=False)
        contribution = jnp.dot(factor_now, panel_low, preferred_element_type=jnp.float32)
        own_couple = couple_back * (row_id == current).astype(jnp.float32)
        summed = lax.psum(contribution + own_couple, "row")
        partial_value = lax.cond(
            row_id == current,
            lambda values: lax.dot_general(
                inverse,
                solved - values,
                first_axes,
                precision=precise,
                preferred_element_type=jnp.float32,
            ),
            lambda values: zero_panel,
            summed,
        )
        value = lax.psum_scatter(partial_value, "col", scatter_dimension=0, tiled=True)
        whole_low = lax.all_gather(value.astype(jnp.bfloat16), "col", axis=0, tiled=True)
        active = row_id == current
        finished = jnp.where(active, value, finished)
        panel_low = jnp.where(active, whole_low, panel_low)
        return (finished, panel_low)

    finished, panel_low = lax.fori_loop(
        0, panel_count, backward, (zero_share, zero_panel.astype(jnp.bfloat16))
    )
    return (finished[None], root_part)


def solution(mesh):
    return jax.shard_map(
        shards,
        mesh=mesh,
        in_specs=(
            P("sub", None, "col", "row"),
            P("sub", None, None),
            P("sub", ("row", "col"), None),
            P("sub", "row", "col", None),
            P("sub", None),
            P("col", None),
            P("sub", "row", None),
            P("col", None),
        ),
        out_specs=(P("sub", ("row", "col"), None), P("col", None)),
        check_vma=False,
    )
```

profile of v0, /device:TPU:32, one launch (start us, length us, event | category | flops | bytes accessed | tf_op | source)
XLA Modules:
  0.0 886.8 jit_solution(2642969435639359948)
XLA Ops:
  8.0 0.7 convert_bitcast_fusion
  8.8 0.1 copy.21
  8.9 0.1 broadcast_in_dim.25
  9.0 0.1 and_select_fusion
  9.1 2.8 fusion.15
  11.9 221.9 %while.37 = (s32[]{:T(128)}, f32[2048,128]{1,0:T(8,128)}, f32[128,128]{0,1:T(8,128)S(1)}, bf16[2,128,2048]{2,1,0:T(8,128)(2,1)}, s32[]{:T(128)}, /*index=5*/f32[...) while((s32[]{:T(128)}, f32[2048,128]{1,0:T(8,128)}, ...), condition=%wide.region_5.6_spmd.clone, body=%wide.region_0.5_spmd.clone.sunk | while | flops 470859776 | bytes 18612512 | solution.py:75
  11.9 0.0 all-reduce.6.cloned.1.call-start
  12.0 1.1 broadcast_select_fusion.7
  13.1 0.0 all-reduce.6.cloned.1.call-update
  13.1 103.1 %all-reduce.6.cloned.1.call-done = f32[2048,128]{1,0:T(8,128)} async-done(((f32[2048,128]{1,0:T(8,128)}), f32[2048,128]{1,0:T(8,128)}) %all-reduce.6.cloned.1.call-update) | async-done | bytes 1048592 | tf_op jit(solution)/shard_map/while/body/eval_jaxpr/psum | solution.py:59
  116.2 3.5 conditional.7
  116.2 3.5 convolution_bitcast_fusion.1
  119.7 3.4 psum.51
  123.1 2.4 convolution_add_fusion.4
  125.5 2.3 broadcast_select_fusion.7
  127.8 0.0 all-reduce.6.cloned.1.call-update
  127.8 98.6 %all-reduce.6.cloned.1.call-done = f32[2048,128]{1,0:T(8,128)} async-done(((f32[2048,128]{1,0:T(8,128)}), f32[2048,128]{1,0:T(8,128)}) %all-reduce.6.cloned.1.call-update) | async-done | bytes 1048592 | tf_op jit(solution)/shard_map/while/body/eval_jaxpr/psum | solution.py:59
  226.4 5.1 psum.51
  231.4 2.4 convolution_add_fusion.4
  233.8 0.2 fusion.19
  234.0 2.9 fusion.16
  237.0 0.9 copy-done.5
  237.9 0.0 all-reduce.4.cloned.1.call-update
  237.9 0.0 reduce-scatter.5.cloned.1.call-start
  238.0 252.3 %all-reduce.4.cloned.1.call-done = f32[1536,128]{1,0:T(8,128)} async-done(((f32[1536,128]{1,0:T(8,128)}), f32[1536,128]{1,0:T(8,128)}) %all-reduce.4.cloned.1.call-update) | async-done | bytes 786448 | tf_op jit(solution)/shard_map/psum | solution.py:89
  490.3 1.9 fusion.24
  492.2 0.8 convolution_bitcast_fusion.2
  493.0 1.2 copy.27
  494.2 0.0 reduce-scatter.5.cloned.1.call-update
  494.2 0.1 copy.24
  494.3 79.0 %reduce-scatter.5.cloned.1.call-done = f32[96,128]{1,0:T(8,128)} async-done(((f32[1536,128]{1,0:T(8,128)}), f32[96,128]{1,0:T(8,128)}) %reduce-scatter.5.cloned.1.call-update) | async-done | bytes 49168 | tf_op jit(solution)/shard_map/reduce_scatter | solution.py:93
  573.4 0.8 convert_element_type.87
  574.2 23.4 %all_gather.13 = bf16[1536,128]{1,0:T(8,128)(2,1)S(1)} all-gather(bf16[96,128]{1,0:T(8,128)(2,1)S(1)} %convert_element_type.87), channel_id=1, replica_groups=mesh['sub'=8,'row'=2,'col'=16] {'col'}, dimensions={0}, use_global_device_ids=true | all-gather | bytes 417792 | tf_op jit(solution)/shard_map/all_gather | solution.py:105
  597.6 1.8 fusion.17
  599.4 0.3 convolution_bitcast_fusion.3
  599.6 0.1 copy.23
  599.7 278.9 %while.38 = (s32[]{:T(128)}, f32[128,128]{0,1:T(8,128)S(1)}, bf16[2048,128]{0,1:T(8,128)(2,1)S(1)}, s32[]{:T(128)}, bf16[2,128,2048]{2,1,0:T(8,128)(2,1)}, /*ind...) while((s32[]{:T(128)}, f32[128,128]{0,1:T(8,128)S(1)}, ...), condition=%wide.region_13.14_spmd.clone, body=%wide.region_8.13_spmd.clone.sunk | while | flops 470663168 | bytes 13697360 | solution.py:139
  599.8 0.0 all-reduce.8.cloned.1.call-start
  599.8 2.0 convolution_add_fusion.5
  601.8 0.0 all-reduce.8.cloned.1.call-update
  601.8 0.0 reduce-scatter.7.cloned.1.call-start
  601.9 29.3 %all-reduce.8.cloned.1.call-done = f32[128,128]{1,0:T(8,128)} async-done(((f32[128,128]{1,0:T(8,128)}), f32[128,128]{1,0:T(8,128)}) %all-reduce.8.cloned.1.call-update) | async-done | bytes 65552 | tf_op jit(solution)/shard_map/while/body/eval_jaxpr/psum | solution.py:119
  631.2 0.1 conditional.8
  631.2 0.1 broadcast_in_dim.1
  631.3 1.0 copy-done.3
  632.3 0.0 reduce-scatter.7.cloned.1.call-update
  632.3 81.8 %reduce-scatter.7.cloned.1.call-done = f32[128,128]{0,1:T(8,128)} async-done(((f32[2048,128]{0,1:T(8,128)}), f32[128,128]{0,1:T(8,128)}) %reduce-scatter.7.cloned.1.call-update) | async-done | bytes 65552 | tf_op jit(solution)/shard_map/while/body/eval_jaxpr/reduce_scatter | solution.py:132
  714.2 0.9 fusion.43
  715.1 24.0 %all_gather.16 = bf16[2048,128]{0,1:T(8,128)(2,1)S(1)} all-gather(bf16[128,128]{0,1:T(8,128)(2,1)S(1)} %get-tuple-element.583), channel_id=1, replica_groups=mesh['sub'=8,'row'=2,'col'=16] {'col'}, dimensions={0}, use_global_device_ids=true | all-gather | bytes 557056 | tf_op jit(solution)/shard_map/while/body/eval_jaxpr/all_gather | solution.py:133
  739.1 0.2 broadcast_select_fusion.9
  739.4 0.0 all-reduce.8.cloned.1.call-start
  739.4 2.0 convolution_add_fusion.5
  741.4 0.0 all-reduce.8.cloned.1.call-update
  741.4 0.0 reduce-scatter.7.cloned.1.call-start
  741.5 29.0 %all-reduce.8.cloned.1.call-done = f32[128,128]{1,0:T(8,128)} async-done(((f32[128,128]{1,0:T(8,128)}), f32[128,128]{1,0:T(8,128)}) %all-reduce.8.cloned.1.call-update) | async-done | bytes 65552 | tf_op jit(solution)/shard_map/while/body/eval_jaxpr/psum | solution.py:119
  770.5 1.9 conditional.8
  770.5 1.9 convolution_bitcast_fusion
  772.4 1.0 copy-done.3
  773.4 0.0 reduce-scatter.7.cloned.1.call-update
  773.4 80.0 %reduce-scatter.7.cloned.1.call-done = f32[128,128]{0,1:T(8,128)} async-done(((f32[2048,128]{0,1:T(8,128)}), f32[128,128]{0,1:T(8,128)}) %reduce-scatter.7.cloned.1.call-update) | async-done | bytes 65552 | tf_op jit(solution)/shard_map/while/body/eval_jaxpr/reduce_scatter | solution.py:132
  853.5 0.9 fusion.43
  854.4 24.0 %all_gather.16 = bf16[2048,128]{0,1:T(8,128)(2,1)S(1)} all-gather(bf16[128,128]{0,1:T(8,128)(2,1)S(1)} %get-tuple-element.583), channel_id=1, replica_groups=mesh['sub'=8,'row'=2,'col'=16] {'col'}, dimensions={0}, use_global_device_ids=true | all-gather | bytes 557056 | tf_op jit(solution)/shard_map/while/body/eval_jaxpr/all_gather | solution.py:133
  878.4 0.2 broadcast_select_fusion.9
  878.6 0.7 copy.25
  (30 shorter events, 0.1 us)
Async XLA Ops:
  8.0 482.3 %copy-start = (f32[96,1536]{1,0:T(8,128)S(1)}, f32[96,1536]{1,0:T(8,128)}, u32[]{:S(2)}) copy-start(f32[96,1536]{1,0:T(8,128)} %param.21) | copy-start | bytes 1769476
  9.1 2.8 copy-start.2
  11.9 221.9 %copy-start.4 = (bf16[1,1,128,1024]{3,2,1,0:T(8,128)(2,1)S(1)}, bf16[1,1,128,1024]{3,2,1,0:T(8,128)(2,1)}, u32[]{:S(2)}) copy-start(bf16[1,1,128,1024]{3,2,1,0:T(8,128)(2,1)} %param.19) | copy-start | bytes 786436
  11.9 222.1 %copy-start.7 = (s32[1,1024]{1,0:T(1,128)S(1)}, s32[1,1024]{1,0:T(1,128)}, u32[]{:S(2)}) copy-start(s32[1,1024]{1,0:T(1,128)} %param.20) | copy-start | bytes 12292
  11.9 104.2 %all-reduce.6.cloned.1.call-start = ((), (), s32[]{:S(2)}) async-start(), calls=%async_computation.4 | async-start | bytes 2097152 | tf_op jit(solution)/shard_map/while/body/eval_jaxpr/psum | solution.py:59
  116.2 6.9 copy-start.1
  125.5 100.9 %all-reduce.6.cloned.1.call-start = ((), (), s32[]{:S(2)}) async-start(), calls=%async_computation.4 | async-start | bytes 2097152 | tf_op jit(solution)/shard_map/while/body/eval_jaxpr/psum | solution.py:59
  226.4 5.1 copy-start.1
  233.8 256.5 %all-reduce.4.cloned.1.call-start = ((), (), s32[]{:S(2)}) async-start(), calls=%async_computation.2 | async-start | bytes 1572864 | tf_op jit(solution)/shard_map/psum | solution.py:89
  234.0 2.9 copy-start.6
  237.0 0.9 copy-start.5
  237.9 335.5 %reduce-scatter.5.cloned.1.call-start = ((), (), s32[]{:S(2)}) async-start(), calls=%async_computation.3 | async-start | bytes 835584 | tf_op jit(solution)/shard_map/reduce_scatter | solution.py:93
  599.8 31.4 %all-reduce.8.cloned.1.call-start = ((), (), s32[]{:S(2)}) async-start(), calls=%async_computation.5 | async-start | bytes 131072 | tf_op jit(solution)/shard_map/while/body/eval_jaxpr/psum | solution.py:119
  601.8 112.3 %reduce-scatter.7.cloned.1.call-start = ((), (), s32[]{:S(2)}) async-start(), calls=%async_computation.6 | async-start | bytes 1114112 | tf_op jit(solution)/shard_map/while/body/eval_jaxpr/reduce_scatter | solution.py:132
  631.3 1.0 copy-start.3
  739.4 31.1 %all-reduce.8.cloned.1.call-start = ((), (), s32[]{:S(2)}) async-start(), calls=%async_computation.5 | async-start | bytes 131072 | tf_op jit(solution)/shard_map/while/body/eval_jaxpr/psum | solution.py:119
  741.4 112.0 %reduce-scatter.7.cloned.1.call-start = ((), (), s32[]{:S(2)}) async-start(), calls=%async_computation.6 | async-start | bytes 1114112 | tf_op jit(solution)/shard_map/while/body/eval_jaxpr/reduce_scatter | solution.py:132
  772.4 1.0 copy-start.3
Sparse Core Ops, SparseCore 0:
  16.4 99.7 all-reduce.5
  129.9 96.4 all-reduce.5
  603.9 27.2 all-reduce.7
  635.0 79.1 reduce-scatter.6
  743.2 27.2 all-reduce.7
  774.3 79.1 reduce-scatter.6
Sparse Core Ops, SparseCore 1:
  239.7 250.5 all-reduce.3
  494.6 78.7 reduce-scatter.4
where the time goes:
time: 888 us; the launch traced here: 887 us
  waiting for transfers between devices  753 us (85%)
  blocking collectives  79.9 us (9%)
  matrix products  24.7 us (3%)
  between operations  15.7 us (2%)
    psum x1, waiting for transfers between devices, shards(): root_rhs = lax.psum(root_term, ('sub', 'row', 'col'))  252 us
    psum x2, waiting for transfers between devices, forward(): panel_total = lax.psum(accumulated, 'col')  202 us
    reduce_scatter x2, waiting for transfers between devices, backward(): lax.psum_scatter(partial_value, 'col', scatter_dimension=0, tiled=True)  162 us
    reduce_scatter x1, waiting for transfers between devices, shards(): lax.psum_scatter(lax.dot_general(root_inverse, root_half, first_axes, pre...  79 us
    psum x2, waiting for transfers between devices, backward(): summed = lax.psum(contribution + own_couple, 'row')  58.3 us
    all_gather x2, blocking collectives, backward(): lax.all_gather(value.astype(jnp.bfloat16), 'col', axis=0, tiled=True)  48.1 us
    all_gather x1, blocking collectives, shards(): lax.all_gather(root_part.astype(jnp.bfloat16), 'col', axis=0, tiled=True)  23.4 us
  transfers between devices with their start and end apart: 8, of which 8 were waited for; matrix products, arithmetic and copies ran while one was open for 0% of the time, Pallas kernels for 0%

commit v1 on v0

--- a/solution.py
+++ b/solution.py
@@ -86,7 +86,7 @@
         lax.dynamic_slice_in_dim(-mapped, slice_start, share_rows, 0) + first_device * root_right
     )
     root_term = lax.dynamic_update_slice_in_dim(-mapped, own_rows, slice_start, 0)
-    root_rhs = lax.psum(root_term, ("sub", "row", "col"))
+    root_rhs = lax.psum(lax.psum(root_term, ("row", "col")), "sub")
     root_half = jnp.dot(
         root_inverse, root_rhs, precision=precise, preferred_element_type=jnp.float32
     )

time: 888 us -> 822 us (0.926)
  waiting for transfers between devices: 753 us -> 687 us
    psum x1 -> x2, waiting for transfers between devices: 252 us -> 189 us  [shards(): root_rhs = lax.psum(lax.psum(root_term, ('row', 'col')), 'sub')]
  transfers between devices with their start and end apart: 8 -> 9, of which waited for: 8 -> 9; matrix products, arithmetic and copies ran while one was open for 0% -> 0% of each run, Pallas kernels for 0% -> 0%
where the time goes in v1:
time: 822 us; the launch traced here: 821 us
  waiting for transfers between devices  687 us (84%)
  blocking collectives  79.9 us (10%)
  matrix products  24.7 us (3%)
  between operations  15.8 us (2%)
    psum x2, waiting for transfers between devices, forward(): panel_total = lax.psum(accumulated, 'col')  202 us
    psum x2, waiting for transfers between devices, shards(): root_rhs = lax.psum(lax.psum(root_term, ('row', 'col')), 'sub')  189 us
    reduce_scatter x2, waiting for transfers between devices, backward(): lax.psum_scatter(partial_value, 'col', scatter_dimension=0, tiled=True)  162 us
    reduce_scatter x1, waiting for transfers between devices, shards(): lax.psum_scatter(lax.dot_general(root_inverse, root_half, first_axes, pre...  76.6 us
    psum x2, waiting for transfers between devices, backward(): summed = lax.psum(contribution + own_couple, 'row')  58.3 us
    all_gather x2, blocking collectives, backward(): lax.all_gather(value.astype(jnp.bfloat16), 'col', axis=0, tiled=True)  48.1 us
    all_gather x1, blocking collectives, shards(): lax.all_gather(root_part.astype(jnp.bfloat16), 'col', axis=0, tiled=True)  23.4 us
  transfers between devices with their start and end apart: 9, of which 9 were waited for; matrix products, arithmetic and copies ran while one was open for 0% of the time, Pallas kernels for 0%

profile of v1, /device:TPU:32, one launch (start us, length us, event | category | flops | bytes accessed | tf_op | source)
XLA Modules:
  0.0 821.1 jit_solution(4670066209806554538)
XLA Ops:
  8.0 0.7 convert_bitcast_fusion
  8.8 0.1 copy.21
  8.9 0.1 broadcast_in_dim.25
  9.0 0.1 and_select_fusion
  9.1 2.8 fusion.15
  11.9 221.9 %while.37 = (s32[]{:T(128)}, f32[2048,128]{1,0:T(8,128)}, f32[128,128]{0,1:T(8,128)S(1)}, bf16[2,128,2048]{2,1,0:T(8,128)(2,1)}, s32[]{:T(128)}, /*index=5*/f32[...) while((s32[]{:T(128)}, f32[2048,128]{1,0:T(8,128)}, ...), condition=%wide.region_5.6_spmd.clone, body=%wide.region_0.5_spmd.clone.sunk | while | flops 470859776 | bytes 18612512 | solution.py:75
  11.9 0.0 all-reduce.9.cloned.1.call-start
  12.0 1.1 broadcast_select_fusion.7
  13.1 103.1 %all-reduce.9.cloned.1.call-done = f32[2048,128]{1,0:T(8,128)} async-done(((f32[2048,128]{1,0:T(8,128)}), f32[2048,128]{1,0:T(8,128)}) %all-reduce.9.cloned.1.call-update) | async-done | bytes 1048592 | tf_op jit(solution)/shard_map/while/body/eval_jaxpr/psum | solution.py:59
  116.2 3.5 conditional.7
  116.2 3.5 convolution_bitcast_fusion.1
  119.7 3.4 psum.59
  123.1 2.4 convolution_add_fusion.4
  125.5 2.3 broadcast_select_fusion.7
  127.8 98.5 %all-reduce.9.cloned.1.call-done = f32[2048,128]{1,0:T(8,128)} async-done(((f32[2048,128]{1,0:T(8,128)}), f32[2048,128]{1,0:T(8,128)}) %all-reduce.9.cloned.1.call-update) | async-done | bytes 1048592 | tf_op jit(solution)/shard_map/while/body/eval_jaxpr/psum | solution.py:59
  226.3 5.1 psum.59
  231.4 2.4 convolution_add_fusion.4
  233.8 0.2 fusion.19
  234.0 2.9 fusion.16
  237.0 0.9 copy-done.5
  237.9 0.0 all-reduce.5.cloned.1.call-update
  237.9 0.0 all-reduce.7.cloned.1.call-start
  238.0 112.6 %all-reduce.5.cloned.1.call-done = f32[1536,128]{1,0:T(8,128)} async-done(((f32[1536,128]{1,0:T(8,128)}), f32[1536,128]{1,0:T(8,128)}) %all-reduce.5.cloned.1.call-update) | async-done | bytes 786448 | tf_op jit(solution)/shard_map/psum | solution.py:89
  350.6 0.0 all-reduce.7.cloned.1.call-update
  350.6 0.0 reduce-scatter.5.cloned.1.call-start
  350.7 76.2 %all-reduce.7.cloned.1.call-done = f32[1536,128]{1,0:T(8,128)} async-done(((f32[1536,128]{1,0:T(8,128)}), f32[1536,128]{1,0:T(8,128)}) %all-reduce.7.cloned.1.call-update) | async-done | bytes 786448 | tf_op jit(solution)/shard_map/psum | solution.py:89
  426.9 1.9 fusion.24
  428.8 0.8 convolution_bitcast_fusion.2
  429.6 1.2 copy.27
  430.8 0.0 reduce-scatter.5.cloned.1.call-update
  430.8 0.1 copy.24
  430.9 76.6 %reduce-scatter.5.cloned.1.call-done = f32[96,128]{1,0:T(8,128)} async-done(((f32[1536,128]{1,0:T(8,128)}), f32[96,128]{1,0:T(8,128)}) %reduce-scatter.5.cloned.1.call-update) | async-done | bytes 49168 | tf_op jit(solution)/shard_map/reduce_scatter | solution.py:93
  507.5 0.8 convert_element_type.87
  508.4 23.4 %all_gather.13 = bf16[1536,128]{1,0:T(8,128)(2,1)S(1)} all-gather(bf16[96,128]{1,0:T(8,128)(2,1)S(1)} %convert_element_type.87), channel_id=1, replica_groups=mesh['sub'=8,'row'=2,'col'=16] {'col'}, dimensions={0}, use_global_device_ids=true | all-gather | bytes 417792 | tf_op jit(solution)/shard_map/all_gather | solution.py:105
  531.7 1.8 fusion.17
  533.5 0.3 convolution_bitcast_fusion.3
  533.8 0.1 copy.23
  533.9 278.9 %while.38 = (s32[]{:T(128)}, f32[128,128]{0,1:T(8,128)S(1)}, bf16[2048,128]{0,1:T(8,128)(2,1)S(1)}, s32[]{:T(128)}, bf16[2,128,2048]{2,1,0:T(8,128)(2,1)}, /*ind...) while((s32[]{:T(128)}, f32[128,128]{0,1:T(8,128)S(1)}, ...), condition=%wide.region_14.15_spmd.clone, body=%wide.region_9.14_spmd.clone.sunk | while | flops 470663168 | bytes 13697360 | solution.py:139
  533.9 0.0 all-reduce.11.cloned.1.call-start
  534.0 2.0 convolution_add_fusion.5
  536.0 0.0 reduce-scatter.7.cloned.1.call-start
  536.0 29.3 %all-reduce.11.cloned.1.call-done = f32[128,128]{1,0:T(8,128)} async-done(((f32[128,128]{1,0:T(8,128)}), f32[128,128]{1,0:T(8,128)}) %all-reduce.11.cloned.1.call-update) | async-done | bytes 65552 | tf_op jit(solution)/shard_map/while/body/eval_jaxpr/psum | solution.py:119
  565.3 0.1 conditional.8
  565.3 0.1 broadcast_in_dim.1
  565.5 1.0 copy-done.3
  566.5 0.0 reduce-scatter.7.cloned.1.call-update
  566.5 81.8 %reduce-scatter.7.cloned.1.call-done = f32[128,128]{0,1:T(8,128)} async-done(((f32[2048,128]{0,1:T(8,128)}), f32[128,128]{0,1:T(8,128)}) %reduce-scatter.7.cloned.1.call-update) | async-done | bytes 65552 | tf_op jit(solution)/shard_map/while/body/eval_jaxpr/reduce_scatter | solution.py:132
  648.3 0.9 fusion.43
  649.2 24.0 %all_gather.16 = bf16[2048,128]{0,1:T(8,128)(2,1)S(1)} all-gather(bf16[128,128]{0,1:T(8,128)(2,1)S(1)} %get-tuple-element.583), channel_id=1, replica_groups=mesh['sub'=8,'row'=2,'col'=16] {'col'}, dimensions={0}, use_global_device_ids=true | all-gather | bytes 557056 | tf_op jit(solution)/shard_map/while/body/eval_jaxpr/all_gather | solution.py:133
  673.3 0.2 broadcast_select_fusion.9
  673.5 0.0 all-reduce.11.cloned.1.call-start
  673.6 2.0 convolution_add_fusion.5
  675.6 0.0 all-reduce.11.cloned.1.call-update
  675.6 0.0 reduce-scatter.7.cloned.1.call-start
  675.6 29.0 %all-reduce.11.cloned.1.call-done = f32[128,128]{1,0:T(8,128)} async-done(((f32[128,128]{1,0:T(8,128)}), f32[128,128]{1,0:T(8,128)}) %all-reduce.11.cloned.1.call-update) | async-done | bytes 65552 | tf_op jit(solution)/shard_map/while/body/eval_jaxpr/psum | solution.py:119
  704.6 1.9 conditional.8
  704.6 1.9 convolution_bitcast_fusion
  706.5 1.0 copy-done.3
  707.5 0.0 reduce-scatter.7.cloned.1.call-update
  707.6 80.0 %reduce-scatter.7.cloned.1.call-done = f32[128,128]{0,1:T(8,128)} async-done(((f32[2048,128]{0,1:T(8,128)}), f32[128,128]{0,1:T(8,128)}) %reduce-scatter.7.cloned.1.call-update) | async-done | bytes 65552 | tf_op jit(solution)/shard_map/while/body/eval_jaxpr/reduce_scatter | solution.py:132
  787.6 0.9 fusion.43
  788.5 24.0 %all_gather.16 = bf16[2048,128]{0,1:T(8,128)(2,1)S(1)} all-gather(bf16[128,128]{0,1:T(8,128)(2,1)S(1)} %get-tuple-element.583), channel_id=1, replica_groups=mesh['sub'=8,'row'=2,'col'=16] {'col'}, dimensions={0}, use_global_device_ids=true | all-gather | bytes 557056 | tf_op jit(solution)/shard_map/while/body/eval_jaxpr/all_gather | solution.py:133
  812.6 0.2 broadcast_select_fusion.9
  812.8 0.7 copy.25
  (33 shorter events, 0.2 us)
Async XLA Ops:
  8.0 418.9 %copy-start = (f32[96,1536]{1,0:T(8,128)S(1)}, f32[96,1536]{1,0:T(8,128)}, u32[]{:S(2)}) copy-start(f32[96,1536]{1,0:T(8,128)} %param.21) | copy-start | bytes 1769476
  9.1 2.8 copy-start.2
  11.9 221.9 %copy-start.4 = (bf16[1,1,128,1024]{3,2,1,0:T(8,128)(2,1)S(1)}, bf16[1,1,128,1024]{3,2,1,0:T(8,128)(2,1)}, u32[]{:S(2)}) copy-start(bf16[1,1,128,1024]{3,2,1,0:T(8,128)(2,1)} %param.19) | copy-start | bytes 786436
  11.9 222.1 %copy-start.7 = (s32[1,1024]{1,0:T(1,128)S(1)}, s32[1,1024]{1,0:T(1,128)}, u32[]{:S(2)}) copy-start(s32[1,1024]{1,0:T(1,128)} %param.20) | copy-start | bytes 12292
  11.9 104.2 %all-reduce.9.cloned.1.call-start = ((), (), s32[]{:S(2)}) async-start(), calls=%async_computation.5 | async-start | bytes 2097152 | tf_op jit(solution)/shard_map/while/body/eval_jaxpr/psum | solution.py:59
  116.2 6.9 copy-start.1
  125.5 100.9 %all-reduce.9.cloned.1.call-start = ((), (), s32[]{:S(2)}) async-start(), calls=%async_computation.5 | async-start | bytes 2097152 | tf_op jit(solution)/shard_map/while/body/eval_jaxpr/psum | solution.py:59
  226.3 5.1 copy-start.1
  233.8 116.8 %all-reduce.5.cloned.1.call-start = ((), (), s32[]{:S(2)}) async-start(), calls=%async_computation.2 | async-start | bytes 1572864 | tf_op jit(solution)/shard_map/psum | solution.py:89
  234.0 2.9 copy-start.6
  237.0 0.9 copy-start.5
  237.9 189.0 %all-reduce.7.cloned.1.call-start = ((), (), s32[]{:S(2)}) async-start(), calls=%async_computation.3 | async-start | bytes 1572864 | tf_op jit(solution)/shard_map/psum | solution.py:89
  350.6 156.9 %reduce-scatter.5.cloned.1.call-start = ((), (), s32[]{:S(2)}) async-start(), calls=%async_computation.4 | async-start | bytes 835584 | tf_op jit(solution)/shard_map/reduce_scatter | solution.py:93
  533.9 31.4 %all-reduce.11.cloned.1.call-start = ((), (), s32[]{:S(2)}) async-start(), calls=%async_computation.6 | async-start | bytes 131072 | tf_op jit(solution)/shard_map/while/body/eval_jaxpr/psum | solution.py:119
  536.0 112.3 %reduce-scatter.7.cloned.1.call-start = ((), (), s32[]{:S(2)}) async-start(), calls=%async_computation.7 | async-start | bytes 1114112 | tf_op jit(solution)/shard_map/while/body/eval_jaxpr/reduce_scatter | solution.py:132
  565.5 1.0 copy-start.3
  673.5 31.1 %all-reduce.11.cloned.1.call-start = ((), (), s32[]{:S(2)}) async-start(), calls=%async_computation.6 | async-start | bytes 131072 | tf_op jit(solution)/shard_map/while/body/eval_jaxpr/psum | solution.py:119
  675.6 112.0 %reduce-scatter.7.cloned.1.call-start = ((), (), s32[]{:S(2)}) async-start(), calls=%async_computation.7 | async-start | bytes 1114112 | tf_op jit(solution)/shard_map/while/body/eval_jaxpr/reduce_scatter | solution.py:132
  706.5 1.0 copy-start.3
Sparse Core Ops, SparseCore 0:
  16.4 99.7 all-reduce.8
  129.9 96.4 all-reduce.8
  538.0 27.2 all-reduce.10
  569.1 79.1 reduce-scatter.6
  677.3 27.2 all-reduce.10
  708.4 79.1 reduce-scatter.6
Sparse Core Ops, SparseCore 1:
  238.0 112.5 all-reduce.4
  352.8 74.0 all-reduce.6
  431.2 76.3 reduce-scatter.4
